TPU v7x, 256 devices: a whole 4x4x8 slice. The times are simulated.
256 devices in a mesh: xy: 32 (over y_hi, z, core), gz: 8 (over y_lo, x).
Axes of the slice: x: 4, y: 4 (y_hi: 2, y_lo: 2; y = y_hi * 2 + y_lo), z: 8, core: 2. Of those that a mesh axis runs over, the one named last changes fastest.
Arguments:
- positions: float32 [3, 32, 6, 32, 128], P(None, 'xy', None, 'gz'), may hold values from 0 to 1
- cotangent: float32 [3, 32, 6, 32, 128], P(None, 'xy', None, 'gz'), may hold values from -6 to 6
- species: int32 [32, 6, 32, 128], P('xy', None, 'gz'), may hold values from 0 to 7
- counts: int32 [32, 6, 32], P('xy', None, 'gz'), may hold values from 8 to 128, as said below
- amplitude: float32 [8, 8], replicated, may hold values from 0.2 to 2
Outputs:
- position_cotangent: float32 [3, 32, 6, 32, 128], P(None, 'xy', None, 'gz')
- amplitude_grad: float32 [8, 8], replicated
Inputs may be any that keep to these rules, and one draw needn't show every extreme that they name: The live beads of a cell fill its first counts slots; cell (0, 0, 0) holds 128 beads.
All inputs are finite; a program needn't handle non-finite values.
Results may differ from a plain program's by a relative error of at most 0.00021.
Values sent between devices are 32-bit elements; how exact they have to be, the bound alone decides.
No kernel may reach another device: no remote copies, remote signals or barrier semaphores. Data moves between devices by JAX's collectives and lax.ppermute only.
A program may use at most 64 MiB of HBM per device.

v0:
```python
import math

import jax
import jax.numpy as jnp
from jax import lax
from jax.experimental import pallas as pl
from jax.experimental.pallas import tpu as pltpu
from jax.sharding import Mesh
from jax.sharding import PartitionSpec as P

AXES = ("y_hi", "z_ax", "core", "y_lo", "x_ax")
ROW = ("y_lo", "x_ax")
COL = ("y_hi", "z_ax", "core")
NX, NZ = 32, 8
step_size = 0.05
FAR = 1.0e4
NY = 6
ZC = 4
SLOTS = 128
KINDS = 8
SHORT = 32
HOMES = NY * ZC
bf16 = jnp.bfloat16
f32 = jnp.float32


def sublane(shape=(8, SLOTS)):
    return lax.broadcasted_iota(jnp.int32, shape, 0)


def pieces(v):
    high = v.astype(bf16).astype(f32)
    rest = v - high
    mid = rest.astype(bf16).astype(f32)
    return high, mid, rest - mid


def pick(row, lo, hi, value, other):
    return jnp.where((row >= lo) & (row < hi), value, other)


def row_sum(row, lo, hi, value):
    return jnp.sum(pick(row, lo, hi, value, 0.0), axis=0, keepdims=True)


def framed(raw, row, sx, sy, sz):
    shift = jnp.where(row == 0, sx, jnp.where(row == 1, sy, jnp.where(row == 2, sz, 0.0)))
    return raw + shift.astype(f32)


def bead_terms(v, row):
    back = pltpu.roll(v, 3, 0)
    square = row_sum(row, 0, 3, v * v)
    cross = row_sum(row, 3, 6, v * back)
    return back, square, cross


def far_features(v, lhs_ref, feat_ref, slot):
    row = sublane()
    back, square, cross = bead_terms(v, row)
    code = v[6:7]
    ahead = pltpu.roll(v, 5, 0)
    gain = jnp.where(code < 0.0, -FAR, 1.0 - square)
    a = pick(row, 0, 3, ahead, pick(row, 3, 6, back, 0.0))
    ah, am, al = pieces(a)
    qh, qm, ql = pieces(gain)
    rh, rm, rl = pieces(cross)
    one = jnp.where(row == 6, 1.0, 0.0)
    last = row == 7
    lhs = jnp.concatenate(
        [
            jnp.where(last, qh, ah + one),
            jnp.where(last, qm, ah + one),
            jnp.where(last, ql, ah + one),
            jnp.where(last, rh, am),
            jnp.where(last, rm, am),
            jnp.where(last, rl, al),
        ],
        axis=0,
    )
    lhs_ref[slot, :, 0:48] = lhs.astype(bf16).T
    mask = code == row.astype(f32)
    high = v.astype(bf16).astype(f32)
    low = v - high
    rows = [jnp.where(mask, 1.0, 0.0)]
    for part, start in ((high, 0), (low, 0), (high, 3), (low, 3)):
        for k in range(3):
            rows.append(jnp.where(mask, part[start + k : start + k + 1], 0.0))
    if feat_ref.shape[1] == 128:
        rows += [jnp.where(mask, r, 0.0) for r in (rh, rm, rl)]
    else:
        rows.append(jnp.zeros((8, SLOTS), f32))
    feat_ref[slot] = jnp.concatenate(rows, axis=0).astype(bf16)


def home_features(v, gram_ref, frame_ref, h):
    row = sublane()
    back, square, cross = bead_terms(v, row)
    square = jnp.where(v[6:7] < 0.0, FAR, square)
    u = pick(row, 3, 6, 2.0 * back, jnp.where(row == 6, -square, 0.0))
    p = pick(row, 0, 6, -v, jnp.where(row == 6, cross, 0.0))
    last = jnp.where(row == 7, 1.0, 0.0)
    uh, um, ul = pieces(u)
    ph, pm, pl_ = pieces(p)
    gram_ref[h, :, 0:SLOTS] = jnp.concatenate(
        [uh + last, um + last, ul + last, uh, um, uh], axis=0
    ).astype(bf16)
    gram_ref[h, :, SLOTS : 2 * SLOTS] = jnp.concatenate(
        [ph, pm, pl_, ph + last, pm + last, ph + last], axis=0
    ).astype(bf16)
    frame_ref[h] = jnp.where(row == 7, cross, v)


def is_short(ref):
    kinds = ref[0, 0, 6:7]
    for z in range(ref.shape[0]):
        for y in range(NY):
            kinds = jnp.maximum(kinds, ref[z, y, 6:7])
    lane = lax.broadcasted_iota(jnp.int32, (1, SLOTS), 1)
    return jnp.max(jnp.where(lane < SHORT, -1.0, kinds)) < 0.0


def pair_body(stage, steps, home_ref, far_refs, left_ref, table_ref, before_ref,
              matrix_before_ref, out_ref, matrix_ref, gram_ref, frame_ref, lhs_ref, feat_ref,
              acc_ref, own_ref, moved_ref, moment_ref, kind_ref):
    row = sublane()
    lane = lax.broadcasted_iota(jnp.int32, (8, SLOTS), 1)
    quarter = lane // SHORT
    both = jnp.logical_and
    no = jnp.logical_not

    def far_bead(i, z, ye):
        y = lax.rem(ye + 5, 6)
        return framed(
            far_refs[i][z, y], row, steps[i] - 0.5, (ye - 4).astype(f32), (z - 3).astype(f32)
        )

    def home_bead(z, y):
        return framed(home_ref[z, y], row, -0.5, (y - 3).astype(f32), (z - 2).astype(f32))

    def prepare_whole(i, low=0, high=6):
        @pl.loop(8 * low, 8 * high, unroll=8)
        def _(n):
            far_features(far_bead(i, n // 8, n % 8), lhs_ref, feat_ref, i * 48 + n)

    def prepare_short(i):
        @pl.loop(0, 12, unroll=2)
        def _(n):
            v = far_bead(i, n // 2, n % 2 * 4)
            for j in range(1, 4):
                other = pltpu.roll(far_bead(i, n // 2, n % 2 * 4 + j), SHORT * j, 1)
                v = jnp.where(quarter == j, other, v)
            far_features(v, lhs_ref, feat_ref, i * 48 + n // 2 * 8 + n % 2)

    def prepare_home():
        @pl.loop(0, HOMES, unroll=8)
        def _(h):
            home_features(home_bead(h // 6, h % 6), gram_ref, frame_ref, h)

    def prepare_packed():
        @pl.loop(0, 2 * ZC, unroll=2)
        def _(n):
            z = n // 2
            y = n % 2 * 3
            v = home_bead(z, y)
            for j in (1, 2):
                v = jnp.where(quarter == j, pltpu.roll(home_bead(z, y + j), SHORT * j, 1), v)
            v = jnp.where(quarter == 3, jnp.where(row == 6, -1.0, 0.0), v)
            home_features(v, gram_ref, frame_ref, HOMES + n)

    def gather(h, slots, target_ref):
        gram = gram_ref[h]
        acc = None
        for slot in slots:
            g = jnp.dot(lhs_ref[slot, :, 0:48], gram, preferred_element_type=f32)
            e = jnp.maximum(g[:, :SLOTS], 0.0)
            terms = jnp.concatenate([e * e, e * g[:, SLOTS:]], axis=1)
            high = terms.astype(bf16)
            low = (terms - high.astype(f32)).astype(bf16)
            feat = feat_ref[slot]
            part = jnp.dot(
                jnp.concatenate([feat, feat], axis=1),
                jnp.concatenate([high, low], axis=0),
                preferred_element_type=f32,
            )
            if stage == 0 and acc is None:
                own_ref[h] = part[56:, :SLOTS]
            acc = part if acc is None else acc + part
        target_ref[h] = acc

    def gather_homes(group, tiles, target_ref, first=0, last=HOMES):
        @pl.loop(0, (last - first) // group)
        def _(q):
            for j in range(group):
                h = first + q * group + j
                z = h // 6
                y = h % 6
                gather(h, [(i * 6 + z + dz) * 8 + y + dy for i, dz, dy in tiles], target_ref)

    def gather_short(i, tiles):
        @pl.loop(0, ZC)
        def _(z):
            for y in range(NY):
                slots = [(z + dz) * 8 + y + dy for _, dz, dy in tiles]
                for dz in range(3):
                    for half in range(y // 4, (y + 2) // 4 + 1):
                        slots.append((i * 6 + z + dz) * 8 + half)
                gather(z * 6 + y, slots, acc_ref)

    def gather_packed(i, short, depths, target_ref):
        @pl.loop(0, ZC // 2)
        def _(pair):
            for z in (2 * pair, 2 * pair + 1):
                for t in range(2):
                    cells = range(2) if short else range(3 * t, 3 * t + 5)
                    slots = [(i * 6 + z + dz) * 8 + c for dz in depths for c in cells]
                    gather(HOMES + 2 * z + t, slots, target_ref)

    if stage == 0:
        prepare_whole(0, 1, 6)
        prepare_home()
        gather_homes(6, OWN_HALF, acc_ref)
    else:
        home_short = is_short(home_ref)
        left_short = is_short(left_ref)
        right_short = is_short(far_refs[1])
        moves = both(both(no(home_short), left_short), no(right_short))
        packed_moves = both(home_short, no(right_short))
        pl.when(home_short)(prepare_packed)
    if stage == 1:
        pl.when(left_short)(lambda: prepare_short(0))
        pl.when(no(left_short))(lambda: prepare_whole(0))
        pl.when(moves)(lambda: prepare_whole(1, 0, 4))
        pl.when(packed_moves)(lambda: prepare_whole(1, 0, 5))
        pl.when(no(home_short))(prepare_home)
        pl.when(both(home_short, left_short))(lambda: gather_packed(0, True, range(3), acc_ref))
        pl.when(both(home_short, no(left_short)))(lambda: gather_packed(0, False, range(3), acc_ref))
        pl.when(both(no(home_short), left_short))(lambda: gather_short(0, []))
        pl.when(both(no(home_short), no(left_short)))(lambda: gather_homes(4, whole(0), acc_ref))
        pl.when(moves)(lambda: gather_homes(3, whole(1), moved_ref, 0, HOMES // 2))
        pl.when(packed_moves)(lambda: gather_packed(1, False, (0, 1), moved_ref))
        moment_ref[...] = jnp.zeros_like(moment_ref)
        kind_ref[...] = jnp.zeros_like(kind_ref)
    if stage == 2:
        prepare_whole(0, 0, 5)
        pl.when(right_short)(lambda: prepare_short(1))
        partly = jnp.logical_or(moves, packed_moves)
        pl.when(partly)(lambda: prepare_whole(1, 2, 6))
        pl.when(no(jnp.logical_or(partly, right_short)))(lambda: prepare_whole(1))
        prepare_home()
        pl.when(home_short)(lambda: gather_homes(6, OWN_OTHER, acc_ref))
        pl.when(both(home_short, right_short))(lambda: gather_packed(1, True, range(3), acc_ref))
        pl.when(packed_moves)(lambda: gather_packed(1, False, (2,), acc_ref))
        pl.when(both(no(home_short), right_short))(lambda: gather_short(1, OWN_OTHER))

        @pl.when(moves)
        def _():
            gather_homes(6, OWN_OTHER, acc_ref, 0, HOMES // 2)
            gather_homes(2, OWN_OTHER + whole(1), acc_ref, HOMES // 2)

        pl.when(both(both(no(home_short), no(left_short)), no(right_short)))(
            lambda: gather_homes(3, OWN_OTHER + whole(1), acc_ref)
        )

    table = table_ref[...]
    columns = [jnp.broadcast_to(table[:, s : s + 1], (8, SLOTS)) for s in range(KINDS)]

    def finish(h, m, moved):
        v = frame_ref[h]
        code = v[6:7]
        mix = jnp.zeros((8, SLOTS), f32)
        for s in range(KINDS):
            mix = jnp.where(code == float(s), columns[s], mix)

        def part(f, half):
            return acc_ref[h, 8 * f : 8 * f + 8, half * SLOTS : (half + 1) * SLOTS]

        def every(f, half):
            value = part(f, half)
            if moved:
                value = value + moved_ref[h, 8 * f : 8 * f + 8, half * SLOTS : (half + 1) * SLOTS]
            return value

        def mixed(value):
            return jnp.sum(value * mix, axis=0, keepdims=True)

        def away(f):
            if stage == 0:
                return part(f, 0) - own_ref[h, 8 * f - 56 : 8 * f - 48]
            return part(f, 0)

        c1 = mixed(every(0, 0))
        c2 = mixed(every(0, 1))
        rows = []
        for k in range(3):
            stretch = v[3 + k : 4 + k] * c1 - mixed(every(7 + k, 0) + every(10 + k, 0))
            bend = v[k : k + 1] * c2 - mixed(every(1 + k, 1) + every(4 + k, 1))
            rows.append(step_size * (6.0 * stretch - 24.0 * bend))
        if stage < 2:
            moment = v[7:8] * part(0, 0) + (away(13) + away(14) + away(15))
            for k in range(3):
                moment = moment - v[3 + k : 4 + k] * (part(1 + k, 0) + part(4 + k, 0))
                moment = moment - v[k : k + 1] * (away(7 + k) + away(10 + k))
            moment_ref[m] = moment
            kind_ref[m] = jnp.where(code == row.astype(f32), 1.0, 0.0)
        return rows

    def finish_homes(moved, first=0, last=HOMES):
        @pl.loop(first, last, unroll=6)
        def _(h):
            z = h // 6
            y = h % 6
            rows = finish(h, h, moved)
            for k in range(3):
                if stage == 2:
                    out_ref[k, 0, y, pl.ds(z, 1), :] = rows[k] + before_ref[z, y, k : k + 1]
                else:
                    old = frame_ref[h, 3 + k : 4 + k] if stage == 0 else before_ref[z, y, k : k + 1]
                    out_ref[z, y, k : k + 1] = rows[k] + old

    def finish_packed(moved):
        @pl.loop(0, ZC, unroll=2)
        def _(z):
            for t in range(2):
                rows = finish(HOMES + 2 * z + t, 2 * z + t, moved)
                for j in range(3):
                    y = 3 * t + j
                    for k in range(3):
                        value = pltpu.roll(rows[k], (SLOTS - SHORT * j) % SLOTS, 1) if j else rows[k]
                        value = jnp.where(lane[0:1] < SHORT, value, 0.0)
                        if stage == 2:
                            out_ref[k, 0, y, pl.ds(z, 1), :] += value
                        else:
                            out_ref[z, y, k : k + 1] = before_ref[z, y, k : k + 1] + value

    if stage == 0:
        finish_homes(False)
    elif stage == 1:
        pl.when(moves)(lambda: finish_homes(True, 0, HOMES // 2))
        pl.when(moves)(lambda: finish_homes(False, HOMES // 2))
        pl.when(both(no(home_short), no(moves)))(lambda: finish_homes(False))
        pl.when(packed_moves)(lambda: finish_packed(True))
        pl.when(both(home_short, right_short))(lambda: finish_packed(False))
    else:
        finish_homes(False)
        pl.when(home_short)(lambda: finish_packed(False))

    if stage < 2:
        total = jnp.zeros((8, 8), f32)
        moments = jnp.concatenate([moment_ref[h] for h in range(HOMES)], axis=1)
        kinds = jnp.concatenate([kind_ref[h] for h in range(HOMES)], axis=1).astype(bf16)
        for piece in pieces(moments):
            total = total + lax.dot_general(
                piece.astype(bf16), kinds, (((1,), (1,)), ((), ())), preferred_element_type=f32
            )
        if stage == 1:
            total = total + matrix_before_ref[...]
        matrix_ref[...] = total


def pair_call(stage, steps, home, fars, table, left=None, before=None, matrix_before=None):
    count = len(steps)
    feats = 112 if stage == 2 else 128
    vmem = pl.BlockSpec(memory_space=pltpu.VMEM)
    operands = [home, *fars, table]
    if stage == 2:
        operands.append(left)
    if stage > 0:
        operands.append(before)
    if stage == 1:
        operands.append(matrix_before)
    packed = HOMES if stage == 0 else HOMES + 2 * ZC
    scratch = [
        pltpu.VMEM((packed, 48, 2 * SLOTS), bf16),
        pltpu.VMEM((packed, 8, SLOTS), f32),
        pltpu.VMEM((48 * count, SLOTS, SLOTS), bf16),
        pltpu.VMEM((48 * count, feats, SLOTS), bf16),
        pltpu.VMEM((packed, feats, 2 * SLOTS), f32),
    ]
    if stage == 0:
        scratch.append(pltpu.VMEM((HOMES, 72, SLOTS), f32))
    if stage == 1:
        scratch.append(pltpu.VMEM((packed, feats, 2 * SLOTS), f32))
    if stage < 2:
        scratch += [pltpu.VMEM((HOMES, 8, SLOTS), f32)] * 2

    def body(home_ref, *refs):
        far_refs = refs[:count]
        table_ref = refs[count]
        refs = list(refs[count + 1 :])
        left_ref = refs.pop(0) if stage == 2 else far_refs[0]
        before_ref = refs.pop(0) if stage > 0 else None
        matrix_before_ref = refs.pop(0) if stage == 1 else None
        out_ref = refs.pop(0)
        matrix_ref = refs.pop(0) if stage < 2 else None
        main = refs[:5]
        own_ref = refs[5] if stage == 0 else None
        moved_ref = refs[5] if stage == 1 else None
        sums = refs[6:] if stage < 2 else [None] * 2
        pair_body(stage, steps, home_ref, far_refs, left_ref, table_ref, before_ref,
                  matrix_before_ref, out_ref, matrix_ref, *main, own_ref, moved_ref, *sums)

    if stage == 2:
        out = (jax.ShapeDtypeStruct((3, 1, NY, ZC, SLOTS), f32),)
    else:
        out = (
            jax.ShapeDtypeStruct((ZC, NY, 8, SLOTS), f32),
            jax.ShapeDtypeStruct((8, 8), f32),
        )
    return pl.pallas_call(
        body,
        out_shape=out,
        in_specs=[vmem] * len(operands),
        out_specs=(vmem,) * len(out),
        scratch_shapes=scratch,
        compiler_params=pltpu.CompilerParams(vmem_limit_bytes=48 * 2**20),
        name=("pairs_own", "pairs_left", "pairs_rest")[stage],
    )(*operands)


def pack_body(counts_ref, pos_ref, cot_ref, species_ref, out_ref, low_ref, high_ref):
    lane = lax.broadcasted_iota(jnp.int32, (1, SLOTS), 1)
    for y in range(NY):
        for z in range(ZC):
            rows = [pos_ref[k, 0, y, z : z + 1, :] for k in range(3)]
            rows += [cot_ref[k, 0, y, z : z + 1, :] for k in range(3)]
            kind = jnp.where(lane < counts_ref[0, z, y], species_ref[0, y, z : z + 1, :], -1)
            rows += [kind.astype(f32), jnp.zeros((1, SLOTS), f32)]
            packed = jnp.concatenate(rows, axis=0)
            out_ref[z, y] = packed
            if z == 0:
                low_ref[0, y] = packed
            if z == ZC - 1:
                high_ref[0, y] = packed


def pack(counts, positions, cotangent, species):
    vmem = pl.BlockSpec(memory_space=pltpu.VMEM)
    return pl.pallas_call(
        pack_body,
        out_shape=(
            jax.ShapeDtypeStruct((ZC, NY, 8, SLOTS), f32),
            jax.ShapeDtypeStruct((1, NY, 8, SLOTS), f32),
            jax.ShapeDtypeStruct((1, NY, 8, SLOTS), f32),
        ),
        in_specs=[pl.BlockSpec(memory_space=pltpu.SMEM)] + [vmem] * 3,
        out_specs=(vmem,) * 3,
        name="pack",
    )(counts, positions, cotangent, species)


def move(block, dx, dz):
    pairs = []
    for i in range(NX):
        for j in range(NZ):
            pairs.append((i * NZ + j, (i + dx) % NX * NZ + (j + dz) % NZ))
    return lax.ppermute(block, AXES, pairs)


OWN_HALF = [(0, 1, 1), (0, 1, 2), (0, 2, 0), (0, 2, 1), (0, 2, 2)]
OWN_OTHER = [(0, 1, 0), (0, 0, 0), (0, 0, 1), (0, 0, 2)]


def whole(i):
    return [(i, dz, dy) for dz in range(3) for dy in range(3)]


def per_device(positions, cotangent, species, counts, amplitude):
    table = 0.5 * (amplitude + amplitude.T)
    home, low, high = pack(jnp.swapaxes(counts, 1, 2), positions, cotangent, species)
    below = move(high, 0, 1)
    above = move(low, 0, -1)
    column = jnp.concatenate([below, home, above], axis=0)
    left = move(column, 1, 0)
    right = move(column, -1, 0)
    part, matrix = pair_call(0, (0.0,), home, (column,), table)
    part, matrix = pair_call(
        1, (-1.0, 1.0), home, (left, right), table, before=part, matrix_before=matrix
    )
    sent = jnp.broadcast_to(matrix.reshape(1, KINDS * KINDS), (NX * NZ, KINDS * KINDS))
    sent, part = lax.optimization_barrier((sent, part))
    heard = lax.all_to_all(sent, AXES, 0, 0, tiled=True)
    (out,) = pair_call(2, (0.0, 1.0), home, (column, right), table, left=left, before=part)
    heard, out = lax.optimization_barrier((heard, out))
    matrix = jnp.sum(heard, axis=0).reshape(KINDS, KINDS)
    cells_total = NX * NY * NZ * ZC
    total = 6.0 * (matrix + matrix.T)
    return out, step_size * total / (2.0 * math.sqrt(cells_total / SLOTS))


def solution(mesh):
    finer = Mesh(mesh.devices.reshape(2, 8, 2, 2, 4), AXES)
    in_specs = (
        P(None, COL, None, ROW, None),
        P(None, COL, None, ROW, None),
        P(COL, None, ROW, None),
        P(COL, None, ROW),
        P(),
    )
    return jax.shard_map(
        per_device,
        mesh=finer,
        in_specs=in_specs,
        out_specs=(P(None, COL, None, ROW, None), P()),
        check_vma=False,
    )
```

profile of v0, /device:TPU:1, one launch (start us, length us, event | category | flops | bytes accessed | tf_op | source)
XLA Modules:
  0.0 60.9 jit_solution(14159960153066433076)
XLA Ops:
  0.6 0.0 copy-start.1
  0.6 1.5 %pack.1 = (f32[4,6,8,128]{3,2,1,0:T(8,128)}, f32[1,6,8,128]{3,2,1,0:T(8,128)}, f32[1,6,8,128]{3,2,1,0:T(8,128)}) custom-call(s32[1,4,6]{2,1,0:T(4,128)} %bitcast.12, f32[3,1,6,4,128]{4,3,2,1,0:T(4,128)} %pos_ref.1, f32[3,1,6,4,128]{4,3,2,1,0:T(4,128)} %cot_ref.1, s32[1,6,4,128]{3,2,1,0:T(4,128)} %species_ref.1), custom_call_target="tpu_custom_call" | custom-call | tf_op jit(solution)/shard_map/pack/pallas_call | solution.py:439
  2.2 2.0 %collective-permute-start = (f32[1,6,8,128]{3,2,1,0:T(8,128)}, f32[1,6,8,128]{3,2,1,0:T(8,128)S(1)}, u32[]{:S(2)}, u32[]{:S(2)}) collective-permute-start(f32[1,6,8,128]{3,2,1,0:T(8,128)} %get-tuple-element.14), channel_id=1, source_target_pairs={{0,1},{1,2},{2,3},{3,4},{4,5},{5,6},{6,7},{7,0},{8,9},{9,10},{10,1... | collective-permute-start | bytes 73736 | tf_op jit(solution)/shard_map/ppermute | solution.py:457
  4.2 2.3 %collective-permute-start.1 = (f32[1,6,8,128]{3,2,1,0:T(8,128)}, f32[1,6,8,128]{3,2,1,0:T(8,128)S(1)}, u32[]{:S(2)}, u32[]{:S(2)}) collective-permute-start(f32[1,6,8,128]{3,2,1,0:T(8,128)} %get-tuple-element.15), channel_id=1, source_target_pairs={{0,7},{1,0},{2,1},{3,2},{4,3},{5,4},{6,5},{7,6},{8,15},{9,8},{10,9... | collective-permute-start | bytes 73736 | tf_op jit(solution)/shard_map/ppermute | solution.py:457
  6.5 0.0 copy-done.1
  6.5 0.1 copy.9
  6.6 1.3 %collective-permute-done = f32[1,6,8,128]{3,2,1,0:T(8,128)S(1)} collective-permute-done((f32[1,6,8,128]{3,2,1,0:T(8,128)}, f32[1,6,8,128]{3,2,1,0:T(8,128)S(1)}, u32[]{:S(2)}, u32[]{:S(2)}) %collective-permute-start) | collective-permute-done | bytes 24608 | tf_op jit(solution)/shard_map/ppermute | solution.py:457
  7.9 0.0 copy-start
  7.9 1.0 %constant_dynamic-update-slice_fusion.1 = f32[6,6,8,128]{3,2,1,0:T(8,128)S(1)} fusion(f32[6,6,8,128]{3,2,1,0:T(8,128)S(1)} %constant_dynamic-update-slice_fusion.2, f32[4,6,8,128]{3,2,1,0:T(8,128)} %get-tuple-element.13.home_ref), kind=kLoop, calls=%fused_computation.1 | loop fusion | bytes 196608
  8.9 0.0 collective-permute-done.1
  8.9 3.7 %collective-permute-start.3 = (f32[6,6,8,128]{3,2,1,0:T(8,128)S(1)}, f32[6,6,8,128]{3,2,1,0:T(8,128)S(1)}, u32[]{:S(2)}, u32[]{:S(2)}) collective-permute-start(f32[6,6,8,128]{3,2,1,0:T(8,128)S(1)} %constant_dynamic-update-slice_fusion.refs_0_), channel_id=1, source_target_pairs={{0,248},{1,249},{2,250},{3,251},{4,252},{5,253},{6,254},{7,255},{8... | collective-permute-start | bytes 442376 | tf_op jit(solution)/shard_map/ppermute | solution.py:457
  12.6 0.0 collective-permute-start.2
  12.6 0.0 copy-done
  12.6 7.3 %pairs_own.1 = (f32[4,6,8,128]{3,2,1,0:T(8,128)S(1)}, f32[8,8]{1,0:T(8,128)S(1)}) custom-call(f32[4,6,8,128]{3,2,1,0:T(8,128)S(1)} %copy-done, f32[6,6,8,128]{3,2,1,0:T(8,128)S(1)} %constant_dynamic-update-slice_fusion.refs_0_, f32[8,8]{1,0:T(8,128)S(1)} %fusion.1.refs_1_.refs_2_), custom_call_target="tpu_custom_call" | custom-call | tf_op jit(solution)/shard_map/pairs_own/pallas_call | solution.py:410
  20.0 0.0 collective-permute-done.3.refs_1_
  20.0 0.0 collective-permute-done.2.refs_0_.refs_3_
  20.0 7.6 %pairs_left.1 = (f32[4,6,8,128]{3,2,1,0:T(8,128)S(1)}, f32[8,8]{1,0:T(8,128)S(1)}) custom-call(f32[4,6,8,128]{3,2,1,0:T(8,128)S(1)} %copy-done, f32[6,6,8,128]{3,2,1,0:T(8,128)S(1)} %collective-permute-done.2.refs_0_.refs_3_, f32[6,6,8,128]{3,2,1,0:T(8,128)S(1)} %collective-permute-done.3.refs_1_, f32[8,8]{1,0:T(8,128)S(1)} %fusion.1.refs_1_.refs_2_, ...), custom_call_target="tpu_custom_call" | custom-call | tf_op jit(solution)/shard_map/pairs_left/pallas_call | solution.py:410
  27.6 0.1 broadcast_in_dim.7
  27.7 0.7 %broadcast_in_dim.8 = f32[256,64]{1,0:T(8,128)} broadcast(f32[64]{0:T(128)S(1)} %broadcast_in_dim.7), dimensions={1} | broadcast | bytes 65792 | tf_op jit(solution)/shard_map/broadcast_in_dim | solution.py:480
  28.4 18.9 %all-to-all-start = ((f32[256,1,64]{2,1,0:T(1,128)}), f32[256,1,64]{2,1,0:T(1,128)S(1)}, u32[]{:S(2)}, u32[]{:S(2)}) async-start(f32[256,1,64]{2,1,0:T(1,128)} %bitcast.2), calls=%async_computation | async-start | bytes 262144 | tf_op jit(solution)/shard_map/all_to_all | solution.py:482
  47.3 12.4 %pairs_rest.1 = f32[3,1,6,4,128]{4,3,2,1,0:T(4,128)} custom-call(f32[4,6,8,128]{3,2,1,0:T(8,128)S(1)} %copy-done, f32[6,6,8,128]{3,2,1,0:T(8,128)S(1)} %constant_dynamic-update-slice_fusion.refs_0_, f32[6,6,8,128]{3,2,1,0:T(8,128)S(1)} %collective-permute-done.3.refs_1_, f32[8,8]{1,0:T(8,128)S(1)} %fusion.1.refs_1_.refs_2_, ...), custom_call_target="tpu_custom_call" | custom-call | tf_op jit(solution)/shard_map/pairs_rest/pallas_call | solution.py:410
  59.7 0.4 all-to-all-done
  60.1 0.1 reduce_sum.9
  60.1 0.1 reshape.11
  60.2 0.1 copy.10
  60.3 0.6 fusion
  (3 shorter events, 0.0 us)
Async XLA Ops:
  0.6 5.9 %copy-start.1 = (f32[8,8]{1,0:T(8,128)S(1)}, f32[8,8]{1,0:T(8,128)}, u32[]{:S(2)}) copy-start(f32[8,8]{1,0:T(8,128)} %param.9) | copy-start | bytes 772
  2.2 5.7 %collective-permute-start = (f32[1,6,8,128]{3,2,1,0:T(8,128)}, f32[1,6,8,128]{3,2,1,0:T(8,128)S(1)}, u32[]{:S(2)}, u32[]{:S(2)}) collective-permute-start(f32[1,6,8,128]{3,2,1,0:T(8,128)} %get-tuple-element.14), channel_id=1, source_target_pairs={{0,1},{1,2},{2,3},{3,4},{4,5},{5,6},{6,7},{7,0},{8,9},{9,10},{10,1... | collective-permute-start | bytes 73736 | tf_op jit(solution)/shard_map/ppermute | solution.py:457
  4.2 4.7 %collective-permute-start.1 = (f32[1,6,8,128]{3,2,1,0:T(8,128)}, f32[1,6,8,128]{3,2,1,0:T(8,128)S(1)}, u32[]{:S(2)}, u32[]{:S(2)}) collective-permute-start(f32[1,6,8,128]{3,2,1,0:T(8,128)} %get-tuple-element.15), channel_id=1, source_target_pairs={{0,7},{1,0},{2,1},{3,2},{4,3},{5,4},{6,5},{7,6},{8,15},{9,8},{10,9... | collective-permute-start | bytes 73736 | tf_op jit(solution)/shard_map/ppermute | solution.py:457
  7.9 4.7 %copy-start = (f32[4,6,8,128]{3,2,1,0:T(8,128)S(1)}, f32[4,6,8,128]{3,2,1,0:T(8,128)}, u32[]{:S(2)}) copy-start(f32[4,6,8,128]{3,2,1,0:T(8,128)} %get-tuple-element.13.home_ref) | copy-start | bytes 294916
  8.9 11.1 %collective-permute-start.3 = (f32[6,6,8,128]{3,2,1,0:T(8,128)S(1)}, f32[6,6,8,128]{3,2,1,0:T(8,128)S(1)}, u32[]{:S(2)}, u32[]{:S(2)}) collective-permute-start(f32[6,6,8,128]{3,2,1,0:T(8,128)S(1)} %constant_dynamic-update-slice_fusion.refs_0_), channel_id=1, source_target_pairs={{0,248},{1,249},{2,250},{3,251},{4,252},{5,253},{6,254},{7,255},{8... | collective-permute-start | bytes 442376 | tf_op jit(solution)/shard_map/ppermute | solution.py:457
  12.6 7.4 %collective-permute-start.2 = (f32[6,6,8,128]{3,2,1,0:T(8,128)S(1)}, f32[6,6,8,128]{3,2,1,0:T(8,128)S(1)}, u32[]{:S(2)}, u32[]{:S(2)}) collective-permute-start(f32[6,6,8,128]{3,2,1,0:T(8,128)S(1)} %constant_dynamic-update-slice_fusion.refs_0_), channel_id=1, source_target_pairs={{0,8},{1,9},{2,10},{3,11},{4,12},{5,13},{6,14},{7,15},{8,16},{9,17... | collective-permute-start | bytes 442376 | tf_op jit(solution)/shard_map/ppermute | solution.py:457
  28.4 31.7 %all-to-all-start = ((f32[256,1,64]{2,1,0:T(1,128)}), f32[256,1,64]{2,1,0:T(1,128)S(1)}, u32[]{:S(2)}, u32[]{:S(2)}) async-start(f32[256,1,64]{2,1,0:T(1,128)} %bitcast.2), calls=%async_computation | async-start | bytes 262144 | tf_op jit(solution)/shard_map/all_to_all | solution.py:482
where the time goes:
time: 61.4 us; the launch traced here: 60.9 us
  Pallas kernels  28.9 us (47%)
  starting transfers between devices  27 us (44%)
  local copies, waits for them, and re-layouts  1.96 us (3%)
  waiting for transfers between devices  1.75 us (3%)
  between operations  0.69 us (1%)
  other arithmetic  0.66 us (1%)
    pallas_call x3, Pallas kernels, pair_call(): pl.pallas_call(body, out_shape=out, in_specs=[vmem] * len(operands), out_...  27.3 us
    all_to_all x1, starting transfers between devices, per_device(): heard = lax.all_to_all(sent, AXES, 0, 0, tiled=True)  18.9 us
    ppermute x4, starting transfers between devices, move(): return lax.ppermute(block, AXES, pairs)  8.05 us
    pallas_call x1, Pallas kernels, pack(): pl.pallas_call(pack_body, out_shape=(jax.ShapeDtypeStruct((ZC, NY, 8, SLO...  1.53 us
    ppermute x4, waiting for transfers between devices, move(): return lax.ppermute(block, AXES, pairs)  1.37 us
  transfers between devices with their start and end apart: 5, of which 2 were waited for; matrix products, arithmetic and copies ran while one was open for 2% of the time, Pallas kernels for 32%

commit v1 on v0

--- a/solution.py
+++ b/solution.py
@@ -219,7 +219,7 @@
     if stage == 0:
         prepare_whole(0, 1, 6)
         prepare_home()
-        gather_homes(6, OWN_HALF, acc_ref)
+        gather_homes(8, OWN_HALF, acc_ref)
     else:
         home_short = is_short(home_ref)
         left_short = is_short(left_ref)
@@ -236,8 +236,8 @@
         pl.when(both(home_short, left_short))(lambda: gather_packed(0, True, range(3), acc_ref))
         pl.when(both(home_short, no(left_short)))(lambda: gather_packed(0, False, range(3), acc_ref))
         pl.when(both(no(home_short), left_short))(lambda: gather_short(0, []))
-        pl.when(both(no(home_short), no(left_short)))(lambda: gather_homes(4, whole(0), acc_ref))
-        pl.when(moves)(lambda: gather_homes(3, whole(1), moved_ref, 0, HOMES // 2))
+        pl.when(both(no(home_short), no(left_short)))(lambda: gather_homes(6, whole(0), acc_ref))
+        pl.when(moves)(lambda: gather_homes(6, whole(1), moved_ref, 0, HOMES // 2))
         pl.when(packed_moves)(lambda: gather_packed(1, False, (0, 1), moved_ref))
         moment_ref[...] = jnp.zeros_like(moment_ref)
         kind_ref[...] = jnp.zeros_like(kind_ref)
@@ -256,10 +256,10 @@
         @pl.when(moves)
         def _():
             gather_homes(6, OWN_OTHER, acc_ref, 0, HOMES // 2)
-            gather_homes(2, OWN_OTHER + whole(1), acc_ref, HOMES // 2)
+            gather_homes(4, OWN_OTHER + whole(1), acc_ref, HOMES // 2)
 
         pl.when(both(both(no(home_short), no(left_short)), no(right_short)))(
-            lambda: gather_homes(3, OWN_OTHER + whole(1), acc_ref)
+            lambda: gather_homes(4, OWN_OTHER + whole(1), acc_ref)
         )
 
     table = table_ref[...]

time: 61.4 us -> 60.4 us (0.984); the launches traced: 60.9 us -> 60.6 us
  no operation moved by 1% of the time
where the time goes in v1:
time: 60.4 us; the launch traced here: 60.6 us
  Pallas kernels  28.6 us (47%)
  starting transfers between devices  27 us (45%)
  local copies, waits for them, and re-layouts  1.96 us (3%)
  waiting for transfers between devices  1.75 us (3%)
  between operations  0.69 us (1%)
  other arithmetic  0.66 us (1%)
    pallas_call x3, Pallas kernels, pair_call(): pl.pallas_call(body, out_shape=out, in_specs=[vmem] * len(operands), out_...  27.1 us
    all_to_all x1, starting transfers between devices, per_device(): heard = lax.all_to_all(sent, AXES, 0, 0, tiled=True)  18.9 us
    ppermute x4, starting transfers between devices, move(): return lax.ppermute(block, AXES, pairs)  8.05 us
    pallas_call x1, Pallas kernels, pack(): pl.pallas_call(pack_body, out_shape=(jax.ShapeDtypeStruct((ZC, NY, 8, SLO...  1.53 us
    ppermute x4, waiting for transfers between devices, move(): return lax.ppermute(block, AXES, pairs)  1.37 us
  transfers between devices with their start and end apart: 5, of which 2 were waited for; matrix products, arithmetic and copies ran while one was open for 2% of the time, Pallas kernels for 32%

profile of v1, /device:TPU:1, one launch (start us, length us, event | category | flops | bytes accessed | tf_op | source)
XLA Modules:
  0.0 60.6 jit_solution(13803601296361868227)
XLA Ops:
  0.6 0.0 copy-start.1
  0.6 1.5 %pack.1 = (f32[4,6,8,128]{3,2,1,0:T(8,128)}, f32[1,6,8,128]{3,2,1,0:T(8,128)}, f32[1,6,8,128]{3,2,1,0:T(8,128)}) custom-call(s32[1,4,6]{2,1,0:T(4,128)} %bitcast.12, f32[3,1,6,4,128]{4,3,2,1,0:T(4,128)} %pos_ref.1, f32[3,1,6,4,128]{4,3,2,1,0:T(4,128)} %cot_ref.1, s32[1,6,4,128]{3,2,1,0:T(4,128)} %species_ref.1), custom_call_target="tpu_custom_call" | custom-call | tf_op jit(solution)/shard_map/pack/pallas_call | solution.py:439
  2.2 2.0 %collective-permute-start = (f32[1,6,8,128]{3,2,1,0:T(8,128)}, f32[1,6,8,128]{3,2,1,0:T(8,128)S(1)}, u32[]{:S(2)}, u32[]{:S(2)}) collective-permute-start(f32[1,6,8,128]{3,2,1,0:T(8,128)} %get-tuple-element.14), channel_id=1, source_target_pairs={{0,1},{1,2},{2,3},{3,4},{4,5},{5,6},{6,7},{7,0},{8,9},{9,10},{10,1... | collective-permute-start | bytes 73736 | tf_op jit(solution)/shard_map/ppermute | solution.py:457
  4.2 2.3 %collective-permute-start.1 = (f32[1,6,8,128]{3,2,1,0:T(8,128)}, f32[1,6,8,128]{3,2,1,0:T(8,128)S(1)}, u32[]{:S(2)}, u32[]{:S(2)}) collective-permute-start(f32[1,6,8,128]{3,2,1,0:T(8,128)} %get-tuple-element.15), channel_id=1, source_target_pairs={{0,7},{1,0},{2,1},{3,2},{4,3},{5,4},{6,5},{7,6},{8,15},{9,8},{10,9... | collective-permute-start | bytes 73736 | tf_op jit(solution)/shard_map/ppermute | solution.py:457
  6.5 0.0 copy-done.1
  6.5 0.1 copy.9
  6.6 1.3 %collective-permute-done = f32[1,6,8,128]{3,2,1,0:T(8,128)S(1)} collective-permute-done((f32[1,6,8,128]{3,2,1,0:T(8,128)}, f32[1,6,8,128]{3,2,1,0:T(8,128)S(1)}, u32[]{:S(2)}, u32[]{:S(2)}) %collective-permute-start) | collective-permute-done | bytes 24608 | tf_op jit(solution)/shard_map/ppermute | solution.py:457
  7.9 0.0 copy-start
  7.9 1.0 %constant_dynamic-update-slice_fusion.1 = f32[6,6,8,128]{3,2,1,0:T(8,128)S(1)} fusion(f32[6,6,8,128]{3,2,1,0:T(8,128)S(1)} %constant_dynamic-update-slice_fusion.2, f32[4,6,8,128]{3,2,1,0:T(8,128)} %get-tuple-element.13.home_ref), kind=kLoop, calls=%fused_computation.1 | loop fusion | bytes 196608
  8.9 0.0 collective-permute-done.1
  8.9 3.7 %collective-permute-start.3 = (f32[6,6,8,128]{3,2,1,0:T(8,128)S(1)}, f32[6,6,8,128]{3,2,1,0:T(8,128)S(1)}, u32[]{:S(2)}, u32[]{:S(2)}) collective-permute-start(f32[6,6,8,128]{3,2,1,0:T(8,128)S(1)} %constant_dynamic-update-slice_fusion.refs_0_), channel_id=1, source_target_pairs={{0,248},{1,249},{2,250},{3,251},{4,252},{5,253},{6,254},{7,255},{8... | collective-permute-start | bytes 442376 | tf_op jit(solution)/shard_map/ppermute | solution.py:457
  12.6 0.0 collective-permute-start.2
  12.6 0.0 copy-done
  12.6 7.1 %pairs_own.1 = (f32[4,6,8,128]{3,2,1,0:T(8,128)S(1)}, f32[8,8]{1,0:T(8,128)S(1)}) custom-call(f32[4,6,8,128]{3,2,1,0:T(8,128)S(1)} %copy-done, f32[6,6,8,128]{3,2,1,0:T(8,128)S(1)} %constant_dynamic-update-slice_fusion.refs_0_, f32[8,8]{1,0:T(8,128)S(1)} %fusion.1.refs_1_.refs_2_), custom_call_target="tpu_custom_call" | custom-call | tf_op jit(solution)/shard_map/pairs_own/pallas_call | solution.py:410
  19.7 0.0 collective-permute-done.3.refs_1_
  19.7 0.0 collective-permute-done.2.refs_0_.refs_3_
  19.7 7.6 %pairs_left.1 = (f32[4,6,8,128]{3,2,1,0:T(8,128)S(1)}, f32[8,8]{1,0:T(8,128)S(1)}) custom-call(f32[4,6,8,128]{3,2,1,0:T(8,128)S(1)} %copy-done, f32[6,6,8,128]{3,2,1,0:T(8,128)S(1)} %collective-permute-done.2.refs_0_.refs_3_, f32[6,6,8,128]{3,2,1,0:T(8,128)S(1)} %collective-permute-done.3.refs_1_, f32[8,8]{1,0:T(8,128)S(1)} %fusion.1.refs_1_.refs_2_, ...), custom_call_target="tpu_custom_call" | custom-call | tf_op jit(solution)/shard_map/pairs_left/pallas_call | solution.py:410
  27.3 0.1 broadcast_in_dim.7
  27.4 0.7 %broadcast_in_dim.8 = f32[256,64]{1,0:T(8,128)} broadcast(f32[64]{0:T(128)S(1)} %broadcast_in_dim.7), dimensions={1} | broadcast | bytes 65792 | tf_op jit(solution)/shard_map/broadcast_in_dim | solution.py:480
  28.1 18.9 %all-to-all-start = ((f32[256,1,64]{2,1,0:T(1,128)}), f32[256,1,64]{2,1,0:T(1,128)S(1)}, u32[]{:S(2)}, u32[]{:S(2)}) async-start(f32[256,1,64]{2,1,0:T(1,128)} %bitcast.2), calls=%async_computation | async-start | bytes 262144 | tf_op jit(solution)/shard_map/all_to_all | solution.py:482
  47.0 12.4 %pairs_rest.1 = f32[3,1,6,4,128]{4,3,2,1,0:T(4,128)} custom-call(f32[4,6,8,128]{3,2,1,0:T(8,128)S(1)} %copy-done, f32[6,6,8,128]{3,2,1,0:T(8,128)S(1)} %constant_dynamic-update-slice_fusion.refs_0_, f32[6,6,8,128]{3,2,1,0:T(8,128)S(1)} %collective-permute-done.3.refs_1_, f32[8,8]{1,0:T(8,128)S(1)} %fusion.1.refs_1_.refs_2_, ...), custom_call_target="tpu_custom_call" | custom-call | tf_op jit(solution)/shard_map/pairs_rest/pallas_call | solution.py:410
  59.4 0.4 all-to-all-done
  59.8 0.1 reduce_sum.9
  59.9 0.1 reshape.11
  60.0 0.1 copy.10
  60.0 0.6 fusion
  (3 shorter events, 0.0 us)
Async XLA Ops:
  0.6 5.9 %copy-start.1 = (f32[8,8]{1,0:T(8,128)S(1)}, f32[8,8]{1,0:T(8,128)}, u32[]{:S(2)}) copy-start(f32[8,8]{1,0:T(8,128)} %param.9) | copy-start | bytes 772
  2.2 5.7 %collective-permute-start = (f32[1,6,8,128]{3,2,1,0:T(8,128)}, f32[1,6,8,128]{3,2,1,0:T(8,128)S(1)}, u32[]{:S(2)}, u32[]{:S(2)}) collective-permute-start(f32[1,6,8,128]{3,2,1,0:T(8,128)} %get-tuple-element.14), channel_id=1, source_target_pairs={{0,1},{1,2},{2,3},{3,4},{4,5},{5,6},{6,7},{7,0},{8,9},{9,10},{10,1... | collective-permute-start | bytes 73736 | tf_op jit(solution)/shard_map/ppermute | solution.py:457
  4.2 4.7 %collective-permute-start.1 = (f32[1,6,8,128]{3,2,1,0:T(8,128)}, f32[1,6,8,128]{3,2,1,0:T(8,128)S(1)}, u32[]{:S(2)}, u32[]{:S(2)}) collective-permute-start(f32[1,6,8,128]{3,2,1,0:T(8,128)} %get-tuple-element.15), channel_id=1, source_target_pairs={{0,7},{1,0},{2,1},{3,2},{4,3},{5,4},{6,5},{7,6},{8,15},{9,8},{10,9... | collective-permute-start | bytes 73736 | tf_op jit(solution)/shard_map/ppermute | solution.py:457
  7.9 4.7 %copy-start = (f32[4,6,8,128]{3,2,1,0:T(8,128)S(1)}, f32[4,6,8,128]{3,2,1,0:T(8,128)}, u32[]{:S(2)}) copy-start(f32[4,6,8,128]{3,2,1,0:T(8,128)} %get-tuple-element.13.home_ref) | copy-start | bytes 294916
  8.9 10.8 %collective-permute-start.3 = (f32[6,6,8,128]{3,2,1,0:T(8,128)S(1)}, f32[6,6,8,128]{3,2,1,0:T(8,128)S(1)}, u32[]{:S(2)}, u32[]{:S(2)}) collective-permute-start(f32[6,6,8,128]{3,2,1,0:T(8,128)S(1)} %constant_dynamic-update-slice_fusion.refs_0_), channel_id=1, source_target_pairs={{0,248},{1,249},{2,250},{3,251},{4,252},{5,253},{6,254},{7,255},{8... | collective-permute-start | bytes 442376 | tf_op jit(solution)/shard_map/ppermute | solution.py:457
  12.6 7.1 %collective-permute-start.2 = (f32[6,6,8,128]{3,2,1,0:T(8,128)S(1)}, f32[6,6,8,128]{3,2,1,0:T(8,128)S(1)}, u32[]{:S(2)}, u32[]{:S(2)}) collective-permute-start(f32[6,6,8,128]{3,2,1,0:T(8,128)S(1)} %constant_dynamic-update-slice_fusion.refs_0_), channel_id=1, source_target_pairs={{0,8},{1,9},{2,10},{3,11},{4,12},{5,13},{6,14},{7,15},{8,16},{9,17... | collective-permute-start | bytes 442376 | tf_op jit(solution)/shard_map/ppermute | solution.py:457
  28.1 31.7 %all-to-all-start = ((f32[256,1,64]{2,1,0:T(1,128)}), f32[256,1,64]{2,1,0:T(1,128)S(1)}, u32[]{:S(2)}, u32[]{:S(2)}) async-start(f32[256,1,64]{2,1,0:T(1,128)} %bitcast.2), calls=%async_computation | async-start | bytes 262144 | tf_op jit(solution)/shard_map/all_to_all | solution.py:482
